TPU v7x, 32 devices: a whole 2x2x4 slice. The times are simulated.
32 devices in a mesh: rep: 2 (over x), node: 2 (over core), ep: 8 (over z, y).
Axes of the slice: x: 2, y: 2, z: 4, core: 2. Of those that a mesh axis runs over, the one named last changes fastest.
Arguments:
- activations: bfloat16 [3072, 7168], P(('rep', 'node', 'ep')), parts along dimension 0, may hold values from -6 to 6
- expert_ids: int32 [3072, 8], P(('rep', 'node', 'ep')), parts along dimension 0, may hold values from 0 to 255, all different within a row; in each aligned block of 96 rows (0 to 95, 96 to 191, ...) at most 8 rows name the same one
- route_scores: float32 [3072, 8], P(('rep', 'node', 'ep')), parts along dimension 0, may hold values from 0.05 to 1
- capacity: int32 [256], replicated, may hold values from 6 to 8
- w_gate: bfloat16 [7168, 4096], P(None, ('node', 'ep')), may hold values from -0.0625 to 0.0625
- w_up: bfloat16 [7168, 4096], P(None, ('node', 'ep')), may hold values from -0.0625 to 0.0625
- w_down: bfloat16 [4096, 7168], P(('node', 'ep')), may hold values from -0.125 to 0.125
Outputs:
- mixed_out: bfloat16 [3072, 7168], P(('rep', 'node', 'ep')), parts along dimension 0
There are 2 independent parts, one for each index of `rep`. A program takes and returns all parts, laid end to end along the dimension named above; an argument that names none is the same for every part. Nothing has to cross between parts.
Inputs may be any that keep to these rules, and one draw needn't show every extreme that they name: `expert_ids`: each row names 8 different experts. In each aligned block of 96 rows (the rows of one device) no expert is named by more than 8 rows, and in some block one expert is named by exactly 8 rows.
All inputs are finite; a program needn't handle non-finite values.
Results may differ from a plain program's by a relative error of at most 0.007.
Values may be sent and summed in bfloat16 or wider, within the bound.
No kernel may reach another device: no remote copies, remote signals or barrier semaphores. Data moves between devices by JAX's collectives and lax.ppermute only.
A program may use at most 128 MiB of HBM per device.

v0:
```python
import jax
import jax.numpy as jnp
from jax import lax
from jax.sharding import PartitionSpec as P

TOPK = 8
SHARDS = 8
SEND_CAP = 8


def shards(activations, expert_ids, route_scores, capacity, w_gate, w_up, w_down):
    n_node = lax.axis_size("node")
    n_ep = lax.axis_size("ep")
    window = n_node * (n_ep // SHARDS)
    tok_rows = activations.shape[0]
    model_width = activations.shape[1]
    send_cap = SEND_CAP
    route_weight = (2.5 * route_scores / jnp.sum(route_scores, axis=1, keepdims=True)).astype(
        jnp.bfloat16
    )
    flat_ids = expert_ids.reshape(-1)
    expert_iota = jnp.arange(window, dtype=jnp.int32)
    onehot = (flat_ids[:, None] == expert_iota[None, :]).astype(jnp.int32)
    running = jnp.cumsum(onehot, axis=0)
    ranking = jnp.sum(onehot * running, axis=1) - 1
    limits = jnp.sum(onehot * capacity[:window][None, :], axis=1)
    is_live = (flat_ids < window) & (ranking < limits)
    slot_index = jnp.where(is_live, ranking * window + flat_ids, -1).reshape(tok_rows, TOPK)
    positions = jnp.arange(send_cap * window, dtype=jnp.int32)
    matches = slot_index[:, :, None] == positions[None, None, :]
    select = jnp.any(matches, axis=1).astype(jnp.bfloat16)
    combine_w = jnp.sum(
        jnp.where(matches, route_weight[:, :, None].astype(jnp.float32), 0.0), axis=1
    ).astype(jnp.bfloat16)
    expert_rows = lax.dot_general(
        select, activations, (((0,), (0,)), ((), ())), preferred_element_type=jnp.float32
    ).astype(jnp.bfloat16)
    copies = jnp.broadcast_to(
        expert_rows.reshape(send_cap, window, 1, model_width),
        (send_cap, window, SHARDS, model_width),
    )
    copies = copies.reshape(send_cap, window * SHARDS * model_width)
    received = lax.all_to_all(copies, ("node", "ep"), split_axis=1, concat_axis=0, tiled=True)
    gate_act = jnp.dot(received, w_gate, preferred_element_type=jnp.float32)
    up_act = jnp.dot(received, w_up, preferred_element_type=jnp.float32)
    inner_act = (jax.nn.silu(gate_act) * up_act).astype(jnp.bfloat16)
    partial_value = jnp.dot(inner_act, w_down, preferred_element_type=jnp.float32).astype(
        jnp.bfloat16
    )
    returned = lax.all_to_all(
        partial_value, ("node", "ep"), split_axis=0, concat_axis=1, tiled=True
    )
    summed = jnp.sum(
        returned.reshape(send_cap, window, SHARDS, model_width).astype(jnp.float32), axis=2
    )
    expert_out = summed.astype(jnp.bfloat16).reshape(send_cap * window, model_width)
    mixed_out = jnp.dot(combine_w, expert_out, preferred_element_type=jnp.float32)
    return mixed_out.astype(jnp.bfloat16)


def solution(mesh):
    placed = (
        P(("rep", "node", "ep"), None),
        P(("rep", "node", "ep"), None),
        P(("rep", "node", "ep"), None),
        P(),
        P(None, ("node", "ep")),
        P(None, ("node", "ep")),
        P(("node", "ep"), None),
    )
    return jax.shard_map(
        shards,
        mesh=mesh,
        in_specs=placed,
        out_specs=P(("rep", "node", "ep"), None),
        check_vma=False,
    )
```

profile of v0, /device:TPU:0, one launch (start us, length us, event | category | flops | bytes accessed | tf_op | source)
XLA Modules:
  0.0 111.7 jit_solution(11825912123103637743)
XLA Ops:
  0.0 0.0 copy-start
  0.0 0.9 copy.40
  0.9 0.1 eq.42
  1.0 0.1 eq.38
  1.1 0.7 slice.11
  1.8 0.6 reduce-window.6
  2.3 0.2 slice_reduce_fusion
  2.5 0.2 reduce-window.9
  2.7 0.1 add_bitcast_fusion
  2.8 0.1 select_reduce_fusion.1
  2.9 0.1 lt.15
  3.0 0.1 copy.42
  3.1 0.1 mul.36
  3.2 0.1 copy.43
  3.3 0.7 add_select_fusion
  4.0 0.0 copy-done
  4.0 0.3 convolution_convert_fusion.2
  4.3 0.1 broadcast_in_dim.28
  4.4 0.2 broadcast_in_dim.29
  4.6 0.0 copy-start.1
  4.6 51.5 %all_to_all.35 = bf16[8,16,7168]{2,0,1:T(8,128)(2,1)S(1)} all-to-all(bf16[8,16,7168]{2,0,1:T(8,128)(2,1)S(1)} %bitcast.42), channel_id=1, replica_groups=mesh['rep'=2,'node'=2,'ep'=8] {'node','ep'}, dimensions={1} | all-to-all | bytes 3670016 | tf_op jit(solution)/shard_map/all_to_all | solution.py:43
  56.1 0.0 copy-done.1
  56.2 0.7 fusion.3
  56.8 6.5 %fusion = bf16[16,8,7168]{2,1,0:T(8,128)(2,1)} fusion(bf16[256,7168]{1,0:T(8,128)(2,1)} %param.13, bf16[7168,256]{1,0:T(8,128)(2,1)} %param.12, bf16[8,16,7168]{2,0,1:T(8,128)(2,1)S(1)} %all_to_all.35, f32[128,256]{1,0:T(8,128)S(1)} %fusion.3), kind=kOutput, calls=%fused_computation.2 | convolution fusion | flops 940638208 | bytes 11141120 | tf_op jit(solution)/shard_map/dot_general | solution.py:47
  63.4 0.0 copy-start.2
  63.4 3.8 %all-to-all-start.1 = ((bf16[16,8,7168]{2,1,0:T(8,128)(2,1)}), bf16[16,8,7168]{2,1,0:T(8,128)(2,1)S(1)}, u32[]{:S(2)}, u32[]{:S(2)}) async-start(bf16[16,8,7168]{2,1,0:T(8,128)(2,1)} %fusion), calls=%async_computation.1 | async-start | bytes 3670016 | tf_op jit(solution)/shard_map/all_to_all | solution.py:50
  67.2 0.0 copy-done.2
  67.3 42.2 %all-to-all-done.1 = bf16[16,8,7168]{2,1,0:T(8,128)(2,1)S(1)} async-done(((bf16[16,8,7168]{2,1,0:T(8,128)(2,1)}), bf16[16,8,7168]{2,1,0:T(8,128)(2,1)S(1)}, u32[]{:S(2)}, u32[]{:S(2)}) %all-to-all-start.1) | async-done | bytes 1835040 | tf_op jit(solution)/shard_map/all_to_all | solution.py:50
  109.5 0.2 bitcast_reduce_fusion
  109.8 0.2 copy.45
  110.0 0.1 reshape.59
  110.1 1.6 %convolution_convert_fusion.1 = bf16[96,7168]{1,0:T(8,128)(2,1)} fusion(bf16[16,7168]{1,0:T(8,128)(2,1)S(1)} %reshape.59, bf16[96,16]{0,1:T(8,128)(2,1)S(1)} %select_reduce_fusion), kind=kOutput, calls=%fused_computation.1 | convolution fusion | flops 22708224 | bytes 1608704 | tf_op jit(solution)/shard_map/dot_general | solution.py:57
  (8 shorter events, 0.1 us)
Async XLA Ops:
  0.0 4.0 %copy-start = (bf16[96,7168]{1,0:T(8,128)(2,1)S(1)}, bf16[96,7168]{1,0:T(8,128)(2,1)}, u32[]{:S(2)}) copy-start(bf16[96,7168]{1,0:T(8,128)(2,1)} %param.7) | copy-start | bytes 4128772
  4.6 51.5 %copy-start.1 = (bf16[7168,256]{1,0:T(8,128)(2,1)S(1)}, bf16[7168,256]{1,0:T(8,128)(2,1)}, u32[]{:S(2)}) copy-start(bf16[7168,256]{1,0:T(8,128)(2,1)} %param.11) | copy-start | bytes 11010052
  63.4 3.9 %copy-start.2 = (f32[96,8]{0,1:T(8,128)S(1)}, f32[96,8]{0,1:T(8,128)}, u32[]{:S(2)}) copy-start(f32[96,8]{0,1:T(8,128)} %param.9) | copy-start | bytes 9220
  63.4 46.1 %all-to-all-start.1 = ((bf16[16,8,7168]{2,1,0:T(8,128)(2,1)}), bf16[16,8,7168]{2,1,0:T(8,128)(2,1)S(1)}, u32[]{:S(2)}, u32[]{:S(2)}) async-start(bf16[16,8,7168]{2,1,0:T(8,128)(2,1)} %fusion), calls=%async_computation.1 | async-start | bytes 3670016 | tf_op jit(solution)/shard_map/all_to_all | solution.py:50
where the time goes:
time: 112 us
  blocking collectives  51.5 us (46%)
  waiting for transfers between devices  42.2 us (38%)
  matrix products  9.13 us (8%)
  starting transfers between devices  3.84 us (3%)
  local copies, waits for them, and re-layouts  2.92 us (3%)
  other arithmetic  1.94 us (2%)
    all_to_all x1, blocking collectives, shards(): lax.all_to_all(copies, ('node', 'ep'), split_axis=1, concat_axis=0, tiled...  51.5 us
    all_to_all x1, waiting for transfers between devices, shards(): lax.all_to_all(partial_value, ('node', 'ep'), split_axis=0, concat_axis=1...  42.2 us
    dot_general x1, matrix products, shards(): jnp.dot(inner_act, w_down, preferred_element_type=jnp.float32)  6.55 us
    all_to_all x1, starting transfers between devices, shards(): lax.all_to_all(partial_value, ('node', 'ep'), split_axis=0, concat_axis=1...  3.84 us
  transfers between devices with their start and end apart: 1, of which 1 were waited for; matrix products, arithmetic and copies ran while one was open for 0% of the time, Pallas kernels for 0%

commit v1 on v0

--- a/solution.py
+++ b/solution.py
@@ -47,8 +47,14 @@
     partial_value = jnp.dot(inner_act, w_down, preferred_element_type=jnp.float32).astype(
         jnp.bfloat16
     )
-    returned = lax.all_to_all(
-        partial_value, ("node", "ep"), split_axis=0, concat_axis=1, tiled=True
+    returned = jnp.concatenate(
+        lax.all_to_all(
+            jnp.stack(jnp.split(partial_value, lax.axis_size(("node", "ep")), axis=0)),
+            ("node", "ep"),
+            0,
+            0,
+        ),
+        axis=1,
     )
     summed = jnp.sum(
         returned.reshape(send_cap, window, SHARDS, model_width).astype(jnp.float32), axis=2

time: 112 us -> 137 us (1.22)
  local copies, waits for them, and re-layouts: 2.92 us -> 27.7 us
    unnamed x7 -> x22, local copies, waits for them, and re-layouts: 0.9 us -> 24.2 us
    another operation x0 -> x1, local copies, waits for them, and re-layouts: none -> 1.55 us  [shards(): jnp.stack(jnp.split(partial_value, lax.axis_size(('node', 'ep')), axis=0))]
where the time goes in v1:
time: 137 us
  blocking collectives  51.5 us (38%)
  waiting for transfers between devices  42.2 us (31%)
  local copies, waits for them, and re-layouts  27.7 us (20%)
  matrix products  9.13 us (7%)
  starting transfers between devices  3.84 us (3%)
  other arithmetic  1.94 us (1%)
    all_to_all x1, blocking collectives, shards(): lax.all_to_all(copies, ('node', 'ep'), split_axis=1, concat_axis=0, tiled...  51.5 us
    all_to_all x1, waiting for transfers between devices, shards(): lax.all_to_all(jnp.stack(jnp.split(partial_value, lax.axis_size(('node',...  42.2 us
    unnamed x22, local copies, waits for them, and re-layouts  24.2 us
    dot_general x1, matrix products, shards(): jnp.dot(inner_act, w_down, preferred_element_type=jnp.float32)  6.55 us
    all_to_all x1, starting transfers between devices, shards(): lax.all_to_all(jnp.stack(jnp.split(partial_value, lax.axis_size(('node',...  3.84 us
  transfers between devices with their start and end apart: 1, of which 1 were waited for; matrix products, arithmetic and copies ran while one was open for 0% of the time, Pallas kernels for 0%

profile of v1, /device:TPU:0, one launch (start us, length us, event | category | flops | bytes accessed | tf_op | source)
XLA Modules:
  0.0 136.5 jit_solution(17642227425404167115)
XLA Ops:
  0.0 0.0 copy-start
  0.0 0.9 copy.40
  0.9 0.1 eq.42
  1.0 0.1 eq.38
  1.1 0.7 slice.11
  1.8 0.6 reduce-window.6
  2.3 0.2 slice_reduce_fusion
  2.5 0.2 reduce-window.9
  2.7 0.1 add_bitcast_fusion
  2.8 0.1 select_reduce_fusion.1
  2.9 0.1 lt.15
  3.0 0.1 copy.42
  3.1 0.1 mul.36
  3.2 0.1 copy.43
  3.3 0.7 add_select_fusion
  4.0 0.0 copy-done
  4.0 0.3 convolution_convert_fusion.2
  4.3 0.1 broadcast_in_dim.28
  4.4 0.2 broadcast_in_dim.29
  4.6 0.0 copy-start.1
  4.6 51.5 %all_to_all.24 = bf16[8,16,7168]{2,0,1:T(8,128)(2,1)S(1)} all-to-all(bf16[8,16,7168]{2,0,1:T(8,128)(2,1)S(1)} %bitcast.104), channel_id=1, replica_groups=mesh['rep'=2,'node'=2,'ep'=8] {'node','ep'}, dimensions={1} | all-to-all | bytes 3670016 | tf_op jit(solution)/shard_map/all_to_all | solution.py:43
  56.1 0.0 copy-done.1
  56.2 0.7 fusion.2
  56.8 6.5 %convolution_convert_fusion = bf16[128,7168]{1,0:T(8,128)(2,1)} fusion(bf16[256,7168]{1,0:T(8,128)(2,1)} %param.13, bf16[7168,256]{1,0:T(8,128)(2,1)} %param.12, bf16[8,16,7168]{2,0,1:T(8,128)(2,1)S(1)} %all_to_all.24, f32[128,256]{1,0:T(8,128)S(1)} %fusion.2), kind=kOutput, calls=%fused_computation | convolution fusion | flops 940638208 | bytes 11141120 | tf_op jit(solution)/shard_map/dot_general | solution.py:47
  63.4 1.5 %fusion.32 = bf16[16,8,7168]{2,1,0:T(8,128)(2,1)} fusion(bf16[128,7168]{1,0:T(8,128)(2,1)} %convolution_convert_fusion), kind=kLoop, calls=%fused_computation.46 | loop fusion | bytes 229376
  64.9 1.6 %fusion.31 = bf16[16,8,7168]{2,1,0:T(8,128)(2,1)} fusion(bf16[16,8,7168]{2,1,0:T(8,128)(2,1)} %fusion.32, bf16[128,7168]{1,0:T(8,128)(2,1)} %convolution_convert_fusion), kind=kLoop, calls=%fused_computation.44 | loop fusion | bytes 229376
  66.5 1.6 %fusion.30 = bf16[16,8,7168]{2,1,0:T(8,128)(2,1)} fusion(bf16[16,8,7168]{2,1,0:T(8,128)(2,1)} %fusion.31, bf16[128,7168]{1,0:T(8,128)(2,1)} %convolution_convert_fusion), kind=kLoop, calls=%fused_computation.42 | loop fusion | bytes 229376
  68.0 1.5 %fusion.29 = bf16[16,8,7168]{2,1,0:T(8,128)(2,1)} fusion(bf16[16,8,7168]{2,1,0:T(8,128)(2,1)} %fusion.30, bf16[128,7168]{1,0:T(8,128)(2,1)} %convolution_convert_fusion), kind=kLoop, calls=%fused_computation.40 | loop fusion | bytes 229376
  69.6 1.5 %fusion.28 = bf16[16,8,7168]{2,1,0:T(8,128)(2,1)} fusion(bf16[16,8,7168]{2,1,0:T(8,128)(2,1)} %fusion.29, bf16[128,7168]{1,0:T(8,128)(2,1)} %convolution_convert_fusion), kind=kLoop, calls=%fused_computation.38 | loop fusion | bytes 229376
  71.1 1.5 %fusion.27 = bf16[16,8,7168]{2,1,0:T(8,128)(2,1)} fusion(bf16[16,8,7168]{2,1,0:T(8,128)(2,1)} %fusion.28, bf16[128,7168]{1,0:T(8,128)(2,1)} %convolution_convert_fusion), kind=kLoop, calls=%fused_computation.36 | loop fusion | bytes 229376
  72.7 1.6 %fusion.26 = bf16[16,8,7168]{2,1,0:T(8,128)(2,1)} fusion(bf16[16,8,7168]{2,1,0:T(8,128)(2,1)} %fusion.27, bf16[128,7168]{1,0:T(8,128)(2,1)} %convolution_convert_fusion), kind=kLoop, calls=%fused_computation.34 | loop fusion | bytes 229376
  74.2 1.5 %fusion.25 = bf16[16,8,7168]{2,1,0:T(8,128)(2,1)} fusion(bf16[16,8,7168]{2,1,0:T(8,128)(2,1)} %fusion.26, bf16[128,7168]{1,0:T(8,128)(2,1)} %convolution_convert_fusion), kind=kLoop, calls=%fused_computation.32 | loop fusion | bytes 229376
  75.8 1.6 %fusion.24 = bf16[16,8,7168]{2,1,0:T(8,128)(2,1)} fusion(bf16[16,8,7168]{2,1,0:T(8,128)(2,1)} %fusion.25, bf16[128,7168]{1,0:T(8,128)(2,1)} %convolution_convert_fusion), kind=kLoop, calls=%fused_computation.30 | loop fusion | bytes 229376
  77.3 1.5 %fusion.23 = bf16[16,8,7168]{2,1,0:T(8,128)(2,1)} fusion(bf16[16,8,7168]{2,1,0:T(8,128)(2,1)} %fusion.24, bf16[128,7168]{1,0:T(8,128)(2,1)} %convolution_convert_fusion), kind=kLoop, calls=%fused_computation.28 | loop fusion | bytes 229376
  78.9 1.6 %fusion.22 = bf16[16,8,7168]{2,1,0:T(8,128)(2,1)} fusion(bf16[16,8,7168]{2,1,0:T(8,128)(2,1)} %fusion.23, bf16[128,7168]{1,0:T(8,128)(2,1)} %convolution_convert_fusion), kind=kLoop, calls=%fused_computation.26 | loop fusion | bytes 229376
  80.4 1.6 %fusion.21 = bf16[16,8,7168]{2,1,0:T(8,128)(2,1)} fusion(bf16[16,8,7168]{2,1,0:T(8,128)(2,1)} %fusion.22, bf16[128,7168]{1,0:T(8,128)(2,1)} %convolution_convert_fusion), kind=kLoop, calls=%fused_computation.24 | loop fusion | bytes 229376
  82.0 1.5 %fusion.20 = bf16[16,8,7168]{2,1,0:T(8,128)(2,1)} fusion(bf16[16,8,7168]{2,1,0:T(8,128)(2,1)} %fusion.21, bf16[128,7168]{1,0:T(8,128)(2,1)} %convolution_convert_fusion), kind=kLoop, calls=%fused_computation.22 | loop fusion | bytes 229376
  83.5 1.6 %fusion.19 = bf16[16,8,7168]{2,1,0:T(8,128)(2,1)} fusion(bf16[16,8,7168]{2,1,0:T(8,128)(2,1)} %fusion.20, bf16[128,7168]{1,0:T(8,128)(2,1)} %convolution_convert_fusion), kind=kLoop, calls=%fused_computation.20 | loop fusion | bytes 229376
  85.1 1.6 %fusion.18 = bf16[16,8,7168]{2,1,0:T(8,128)(2,1)} fusion(bf16[16,8,7168]{2,1,0:T(8,128)(2,1)} %fusion.19, bf16[128,7168]{1,0:T(8,128)(2,1)} %convolution_convert_fusion), kind=kLoop, calls=%fused_computation.18 | loop fusion | bytes 229376
  86.7 1.5 %fusion.17 = bf16[16,8,7168]{2,1,0:T(8,128)(2,1)} fusion(bf16[16,8,7168]{2,1,0:T(8,128)(2,1)} %fusion.18, bf16[128,7168]{1,0:T(8,128)(2,1)} %convolution_convert_fusion), kind=kLoop, calls=%fused_computation.16 | loop fusion | bytes 229376 | tf_op jit(solution)/shard_map/stack | solution.py:52
  88.2 0.0 copy-start.2
  88.2 3.8 %all-to-all-start.1 = ((bf16[16,8,7168]{2,1,0:T(8,128)(2,1)}), bf16[16,8,7168]{2,1,0:T(8,128)(2,1)S(1)}, u32[]{:S(2)}, u32[]{:S(2)}) async-start(bf16[16,8,7168]{2,1,0:T(8,128)(2,1)} %fusion.17), calls=%async_computation.1 | async-start | bytes 3670016 | tf_op jit(solution)/shard_map/all_to_all | solution.py:51
  92.1 0.0 copy-done.2
  92.1 42.2 %all-to-all-done.1 = bf16[16,8,7168]{2,1,0:T(8,128)(2,1)S(1)} async-done(((bf16[16,8,7168]{2,1,0:T(8,128)(2,1)}), bf16[16,8,7168]{2,1,0:T(8,128)(2,1)S(1)}, u32[]{:S(2)}, u32[]{:S(2)}) %all-to-all-start.1) | async-done | bytes 1835040 | tf_op jit(solution)/shard_map/all_to_all | solution.py:51
  134.3 0.2 bitcast_reduce_fusion
  134.6 0.2 copy.45
  134.8 0.1 reshape.55
  134.9 1.6 %convolution_convert_fusion.1 = bf16[96,7168]{1,0:T(8,128)(2,1)} fusion(bf16[16,7168]{1,0:T(8,128)(2,1)S(1)} %reshape.55, bf16[96,16]{0,1:T(8,128)(2,1)S(1)} %select_reduce_fusion), kind=kOutput, calls=%fused_computation.1 | convolution fusion | flops 22708224 | bytes 1608704 | tf_op jit(solution)/shard_map/dot_general | solution.py:63
  (8 shorter events, 0.1 us)
Async XLA Ops:
  0.0 4.0 %copy-start = (bf16[96,7168]{1,0:T(8,128)(2,1)S(1)}, bf16[96,7168]{1,0:T(8,128)(2,1)}, u32[]{:S(2)}) copy-start(bf16[96,7168]{1,0:T(8,128)(2,1)} %param.7) | copy-start | bytes 4128772
  4.6 51.5 %copy-start.1 = (bf16[7168,256]{1,0:T(8,128)(2,1)S(1)}, bf16[7168,256]{1,0:T(8,128)(2,1)}, u32[]{:S(2)}) copy-start(bf16[7168,256]{1,0:T(8,128)(2,1)} %param.11) | copy-start | bytes 11010052
  88.2 3.9 %copy-start.2 = (f32[96,8]{0,1:T(8,128)S(1)}, f32[96,8]{0,1:T(8,128)}, u32[]{:S(2)}) copy-start(f32[96,8]{0,1:T(8,128)} %param.9) | copy-start | bytes 9220
  88.2 46.1 %all-to-all-start.1 = ((bf16[16,8,7168]{2,1,0:T(8,128)(2,1)}), bf16[16,8,7168]{2,1,0:T(8,128)(2,1)S(1)}, u32[]{:S(2)}, u32[]{:S(2)}) async-start(bf16[16,8,7168]{2,1,0:T(8,128)(2,1)} %fusion.17), calls=%async_computation.1 | async-start | bytes 3670016 | tf_op jit(solution)/shard_map/all_to_all | solution.py:51
